TPU v7x, 256 devices: a whole 4x4x8 slice. The times are simulated.
256 devices in a mesh: dom: 16 (over y, z_hi, core), orb: 16 (over z_lo, x).
Axes of the slice: x: 4, y: 4, z: 8 (z_hi: 2, z_lo: 4; z = z_hi * 4 + z_lo), core: 2. Of those that a mesh axis runs over, the one named last changes fastest.
Arguments:
- psi: float32 [49152, 2048], P('dom', 'orb'), may hold values from -6 to 6
- rot: float32 [2048, 2048], P(None, 'orb'), may hold values from -0.125 to 0.125
- occ: float32 [2048], P('orb'), may hold values from 0.1 to 2
- v_loc: float32 [49152], P('dom'), may hold values from -1 to 1
Outputs:
- rotated: float32 [49152, 2048], P('dom', 'orb')
- density: float32 [49152], P('dom')
- hpsi: float32 [49152, 2048], P('dom', 'orb')
- band: float32 [2048], P('orb')
All inputs are finite; a program needn't handle non-finite values.
Results may differ from a plain program's by a relative error of at most 0.000075.
Values sent between devices are 32-bit elements; how exact they have to be, the bound alone decides.
A program may use at most 128 MiB of HBM per device.

v0:
```python
import jax
import jax.numpy as jnp
from jax import lax
from jax.sharding import PartitionSpec as P

M = 2048
PLANES_DEV = 3
NY = 8
NZ = 128


def with_halo(cells, sides, width):
    for axis, dim in sides:
        count = lax.axis_size(axis)
        head = lax.slice_in_dim(cells, 0, width, axis=dim)
        tail = lax.slice_in_dim(cells, cells.shape[dim] - width, cells.shape[dim], axis=dim)
        cells = jnp.concatenate(
            [
                lax.ppermute(tail, axis, [(i, (i + 1) % count) for i in range(count)]),
                cells,
                lax.ppermute(head, axis, [((i + 1) % count, i) for i in range(count)]),
            ],
            axis=dim,
        )
    return cells


def shards(psi, rot, occ, v_loc):
    points = psi.shape[0]
    local_m = psi.shape[1]
    rotated = jnp.dot(
        lax.all_gather(psi, "orb", axis=1, tiled=True),
        rot,
        precision=lax.Precision.HIGHEST,
        preferred_element_type=jnp.float32,
    )
    factor = (3.0 / jnp.pi) ** (1.0 / 3.0)
    part_density = jnp.sum(occ[None, :] * rotated * rotated, axis=1) / M
    density = lax.psum(part_density, "orb")
    potential = v_loc - factor * jnp.cbrt(density)
    field = rotated.reshape(PLANES_DEV, NY, NZ, local_m)
    padded = with_halo(field, (("dom", 0),), 1)
    beside = padded[2:] + padded[:-2]
    beside = beside + jnp.roll(field, 1, 1) + jnp.roll(field, -1, 1)
    beside = beside + jnp.roll(field, 1, 2) + jnp.roll(field, -1, 2)
    lap = (beside - 6.0 * field).reshape(points, local_m)
    hpsi = -0.5 * lap + potential[:, None] * rotated
    total_points = points * lax.axis_size("dom")
    band = lax.psum(jnp.sum(rotated * hpsi, axis=0) / total_points, "dom")
    return (rotated, density, hpsi, band)


def solution(mesh):
    placed = (P("dom", "orb"), P(None, "orb"), P("orb"), P("dom"))
    return jax.shard_map(
        shards,
        mesh=mesh,
        in_specs=placed,
        out_specs=(P("dom", "orb"), P("dom"), P("dom", "orb"), P("orb")),
        check_vma=False,
    )
```

profile of v0, /device:TPU:32, one launch (start us, length us, event | category | flops | bytes accessed | tf_op | source)
XLA Modules:
  0.0 473.9 jit_solution(15447638817102200703)
XLA Ops:
  7.2 0.0 copy-start
  7.2 0.0 copy-start.5
  7.2 0.0 all-gather.2.cloned.1.call-start
  7.2 0.7 all-gather.2.cloned.1.call-update
  7.9 279.5 %all-gather.2.cloned.1.call-done = f32[3072,2048]{1,0:T(8,128)} async-done(((f32[3072,128]{1,0:T(8,128)}), f32[3072,2048]{1,0:T(8,128)}) %all-gather.2.cloned.1.call-update) | async-done | bytes 25165840 | tf_op jit(solution)/shard_map/all_gather | solution.py:32
  287.4 0.0 copy-done
  287.4 0.0 copy-done.5
  287.4 23.2 %fusion = (f32[3072]{0:T(1024)S(1)}, f32[3072,128]{1,0:T(8,128)S(1)}) fusion(f32[128]{0:T(128)S(1)} %copy-done.5, f32[3072,2048]{1,0:T(8,128)} %all-gather.2.cloned.1.call-done, f32[2048,128]{1,0:T(8,128)S(1)} %copy-done), kind=kOutput, calls=%fused_computation.1 | convolution fusion | flops 9664852992 | bytes 27800064 | tf_op jit(solution)/shard_map/dot_general | solution.py:31
  310.7 0.0 copy-start.1
  310.7 0.7 fusion.9
  311.4 0.9 fusion.12
  312.3 1.9 fusion.10
  314.1 0.6 broadcast_multiply_fusion
  314.7 72.6 %psum.14 = f32[3072]{0:T(1024)} all-reduce(f32[3072]{0:T(1024)} %broadcast_multiply_fusion), channel_id=1, replica_groups=mesh['dom'=16,'orb'=16] {'orb'}, use_global_device_ids=true, to_apply=%region_1.0 | all-reduce | flops 3072 | bytes 24576 | tf_op jit(solution)/shard_map/psum | solution.py:39
  387.3 0.0 collective-permute-start.1
  387.3 7.8 %collective-permute-start = (f32[1,8,128,128]{3,2,1,0:T(8,128)S(1)}, f32[1,8,128,128]{3,2,1,0:T(8,128)S(1)}, u32[]{:S(2)}, u32[]{:S(2)}) collective-permute-start(f32[1,8,128,128]{3,2,1,0:T(8,128)S(1)} %bitcast.13), channel_id=1, source_target_pairs={{16,0},{32,16},{48,32},{64,48},{80,64},{96,80},{112,96},{128,112},... | collective-permute-start | bytes 1572872 | tf_op jit(solution)/shard_map/ppermute | solution.py:21
  395.1 0.7 multiply_subtract_fusion
  395.8 0.0 copy-start.2
  395.8 0.0 copy-start.3
  395.9 0.0 copy-start.4
  395.9 0.3 fusion.8
  396.2 22.8 %collective-permute-done.1 = f32[1,8,128,128]{3,2,1,0:T(8,128)S(1)} collective-permute-done((f32[1,8,128,128]{3,2,1,0:T(8,128)}, f32[1,8,128,128]{3,2,1,0:T(8,128)S(1)}, u32[]{:S(2)}, u32[]{:S(2)}) %collective-permute-start.1) | collective-permute-done | bytes 524320 | tf_op jit(solution)/shard_map/ppermute | solution.py:19
  419.0 0.0 collective-permute-done
  419.0 0.0 copy-done.2
  419.0 0.0 copy-done.3
  419.0 0.0 copy-done.4
  419.0 1.1 fusion.7
  420.1 0.0 copy-done.1
  420.1 1.6 multiply_reduce_fusion
  421.7 45.3 %psum.15 = f32[128]{0:T(128)} all-reduce(f32[128]{0:T(128)S(1)} %broadcast_multiply_fusion.1), channel_id=1, replica_groups=mesh['dom'=16,'orb'=16] {'dom'}, use_global_device_ids=true, to_apply=%region_3.4 | all-reduce | flops 128 | bytes 1024 | tf_op jit(solution)/shard_map/psum | solution.py:49
  (2 shorter events, 0.0 us)
Async XLA Ops:
  7.2 280.2 %copy-start = (f32[2048,128]{1,0:T(8,128)S(1)}, f32[2048,128]{1,0:T(8,128)}, u32[]{:S(2)}) copy-start(f32[2048,128]{1,0:T(8,128)} %param.5) | copy-start | bytes 3145732
  7.2 280.2 %copy-start.5 = (f32[128]{0:T(128)S(1)}, f32[128]{0:T(128)}, u32[]{:S(2)}) copy-start(f32[128]{0:T(128)} %param.6) | copy-start | bytes 1540
  7.2 280.2 %all-gather.2.cloned.1.call-start = ((), (), s32[]{:S(2)}) async-start(), calls=%async_computation | async-start | bytes 26738688 | tf_op jit(solution)/shard_map/all_gather | solution.py:32
  310.7 109.4 %copy-start.1 = (f32[3072,128]{1,0:T(8,128)}, f32[3072,128]{1,0:T(8,128)S(1)}, u32[]{:S(2)}) copy-start(f32[3072,128]{1,0:T(8,128)S(1)} %get-tuple-element.17) | copy-start | bytes 4718596
  387.3 31.7 %collective-permute-start.1 = (f32[1,8,128,128]{3,2,1,0:T(8,128)}, f32[1,8,128,128]{3,2,1,0:T(8,128)S(1)}, u32[]{:S(2)}, u32[]{:S(2)}) collective-permute-start(f32[1,8,128,128]{3,2,1,0:T(8,128)} %bitcast.14), channel_id=1, source_target_pairs={{0,16},{16,32},{32,48},{48,64},{64,80},{80,96},{96,112},{112,128},... | collective-permute-start | bytes 1572872 | tf_op jit(solution)/shard_map/ppermute | solution.py:19
  387.3 31.7 %collective-permute-start = (f32[1,8,128,128]{3,2,1,0:T(8,128)S(1)}, f32[1,8,128,128]{3,2,1,0:T(8,128)S(1)}, u32[]{:S(2)}, u32[]{:S(2)}) collective-permute-start(f32[1,8,128,128]{3,2,1,0:T(8,128)S(1)} %bitcast.13), channel_id=1, source_target_pairs={{16,0},{32,16},{48,32},{64,48},{80,64},{96,80},{112,96},{128,112},... | collective-permute-start | bytes 1572872 | tf_op jit(solution)/shard_map/ppermute | solution.py:21
  395.8 23.2 %copy-start.2 = (f32[3,7,128,128]{3,2,1,0:T(8,128)S(1)}, f32[3,7,128,128]{3,2,1,0:T(8,128)}, u32[]{:S(2)}) copy-start(f32[3,7,128,128]{3,2,1,0:T(8,128)} %get-tuple-element.10) | copy-start | bytes 4128772
  395.8 23.2 %copy-start.3 = (f32[3,7,128,128]{3,2,1,0:T(8,128)S(1)}, f32[3,7,128,128]{3,2,1,0:T(8,128)}, u32[]{:S(2)}) copy-start(f32[3,7,128,128]{3,2,1,0:T(8,128)} %get-tuple-element.11) | copy-start | bytes 4128772
  395.9 23.1 %copy-start.4 = (f32[3,8,1,128]{3,2,1,0:T(1,128)S(1)}, f32[3,8,1,128]{3,2,1,0:T(1,128)}, u32[]{:S(2)}) copy-start(f32[3,8,1,128]{3,2,1,0:T(1,128)} %get-tuple-element.9) | copy-start | bytes 36868
Sparse Core Ops, SparseCore 0:
  9.7 277.6 all-gather.1
where the time goes:
time: 474 us
  waiting for transfers between devices  303 us (64%)
  blocking collectives  118 us (25%)
  matrix products  23.2 us (5%)
  between operations  14.1 us (3%)
  starting transfers between devices  7.8 us (2%)
    all_gather x1, waiting for transfers between devices, shards(): lax.all_gather(psi, 'orb', axis=1, tiled=True)  279 us
    psum x1, blocking collectives, shards(): density = lax.psum(part_density, 'orb')  72.6 us
    psum x1, blocking collectives, shards(): band = lax.psum(jnp.sum(rotated * hpsi, axis=0) / total_points, 'dom')  45.3 us
    dot_general x1, matrix products, shards(): jnp.dot(lax.all_gather(psi, 'orb', axis=1, tiled=True), rot, precision=la...  23.2 us
    ppermute x1, waiting for transfers between devices, with_halo(): lax.ppermute(tail, axis, [(i, (i + 1) % count) for i in range(count)])  22.8 us
  transfers between devices with their start and end apart: 3, of which 2 were waited for; matrix products, arithmetic and copies ran while one was open for 0% of the time, Pallas kernels for 0%

commit v1 on v0

--- a/solution.py
+++ b/solution.py
@@ -29,7 +29,9 @@
     points = psi.shape[0]
     local_m = psi.shape[1]
     rotated = jnp.dot(
-        lax.all_gather(psi, "orb", axis=1, tiled=True),
+        jnp.concatenate(
+            lax.all_to_all(jnp.stack([psi] * lax.axis_size("orb")), "orb", 0, 0), axis=1
+        ),
         rot,
         precision=lax.Precision.HIGHEST,
         preferred_element_type=jnp.float32,

time: 474 us -> 762 us (1.61)
  blocking collectives: 118 us -> 668 us
  waiting for transfers between devices: 303 us -> 22.8 us
  matrix products: 23.2 us -> 40.9 us
  local copies, waits for them, and re-layouts: 3.84 us -> 17.4 us
  between operations: 14.1 us -> 0.73 us
    all_to_all x0 -> x1, blocking collectives: none -> 551 us  [shards(): lax.all_to_all(jnp.stack([psi] * lax.axis_size('orb')), 'orb', 0, 0)]
    all_gather x1 -> x0, waiting for transfers between devices: 279 us -> none  [shards(): lax.all_gather(psi, 'orb', axis=1, tiled=True)]
    dot_general x1, matrix products: 23.2 us -> 40.9 us  [shards(): jnp.dot(jnp.concatenate(lax.all_to_all(jnp.stack([psi] * lax.axis_size('o...]
    another operation x0 -> x1, local copies, waits for them, and re-layouts: none -> 11.6 us  [shards(): jnp.stack([psi] * lax.axis_size('orb'))]
  transfers between devices with their start and end apart: 3 -> 2, of which waited for: 2 -> 1; matrix products, arithmetic and copies ran while one was open for 0% -> 0% of each run, Pallas kernels for 0% -> 0%
where the time goes in v1:
time: 762 us
  blocking collectives  668 us (88%)
  matrix products  40.9 us (5%)
  waiting for transfers between devices  22.8 us (3%)
  local copies, waits for them, and re-layouts  17.4 us (2%)
  starting transfers between devices  7.76 us (1%)
    all_to_all x1, blocking collectives, shards(): lax.all_to_all(jnp.stack([psi] * lax.axis_size('orb')), 'orb', 0, 0)  551 us
    psum x1, blocking collectives, shards(): density = lax.psum(part_density, 'orb')  69.6 us
    psum x1, blocking collectives, shards(): band = lax.psum(jnp.sum(rotated * hpsi, axis=0) / total_points, 'dom')  47.3 us
    dot_general x1, matrix products, shards(): jnp.dot(jnp.concatenate(lax.all_to_all(jnp.stack([psi] * lax.axis_size('o...  40.9 us
    ppermute x1, waiting for transfers between devices, with_halo(): lax.ppermute(tail, axis, [(i, (i + 1) % count) for i in range(count)])  22.7 us
  transfers between devices with their start and end apart: 2, of which 1 were waited for; matrix products, arithmetic and copies ran while one was open for 0% of the time, Pallas kernels for 0%

profile of v1, /device:TPU:32, one launch (start us, length us, event | category | flops | bytes accessed | tf_op | source)
XLA Modules:
  0.0 762.0 jit_solution(6375569501251871585)
XLA Ops:
  0.6 0.0 copy-start
  0.6 2.0 copy.8
  2.6 11.6 %stack.2 = f32[16,3072,128]{1,2,0:T(8,128)} broadcast(f32[3072,128]{0,1:T(8,128)S(1)} %copy.8), dimensions={1,2} | broadcast | bytes 26738688 | tf_op jit(solution)/shard_map/stack | solution.py:33
  14.3 0.0 copy-start.5
  14.3 551.5 %all_to_all.5 = f32[16,3072,128]{1,2,0:T(8,128)S(1)} all-to-all(f32[16,3072,128]{1,2,0:T(8,128)} %stack.2), channel_id=1, replica_groups=mesh['dom'=16,'orb'=16] {'orb'}, dimensions={0} | all-to-all | bytes 50331648 | tf_op jit(solution)/shard_map/all_to_all | solution.py:33
  565.7 0.0 copy-done
  565.7 0.0 copy-done.5
  565.7 40.9 %fusion = (f32[3072]{0:T(1024)S(1)}, f32[3072,128]{1,0:T(8,128)S(1)}) fusion(f32[128]{0:T(128)S(1)} %copy-done.5, f32[3072,2048]{0,1:T(8,128)S(1)} %bitcast.11, f32[2048,128]{1,0:T(8,128)S(1)} %copy-done), kind=kOutput, calls=%fused_computation.1 | convolution fusion | flops 9664852992 | bytes 27800064 | tf_op jit(solution)/shard_map/dot_general | solution.py:31
  606.7 0.0 copy-start.1
  606.7 0.7 fusion.9
  607.4 0.9 fusion.12
  608.3 1.9 fusion.10
  610.1 0.6 broadcast_multiply_fusion
  610.7 69.6 %psum.14 = f32[3072]{0:T(1024)} all-reduce(f32[3072]{0:T(1024)} %broadcast_multiply_fusion), channel_id=1, replica_groups=mesh['dom'=16,'orb'=16] {'orb'}, use_global_device_ids=true, to_apply=%region_1.0 | all-reduce | flops 3072 | bytes 24576 | tf_op jit(solution)/shard_map/psum | solution.py:41
  680.3 0.0 collective-permute-start.1
  680.3 7.8 %collective-permute-start = (f32[1,8,128,128]{3,2,1,0:T(8,128)S(1)}, f32[1,8,128,128]{3,2,1,0:T(8,128)S(1)}, u32[]{:S(2)}, u32[]{:S(2)}) collective-permute-start(f32[1,8,128,128]{3,2,1,0:T(8,128)S(1)} %bitcast.17), channel_id=1, source_target_pairs={{16,0},{32,16},{48,32},{64,48},{80,64},{96,80},{112,96},{128,112},... | collective-permute-start | bytes 1572872 | tf_op jit(solution)/shard_map/ppermute | solution.py:21
  688.1 0.7 multiply_subtract_fusion
  688.8 0.0 copy-start.2
  688.8 0.0 copy-start.3
  688.9 0.0 copy-start.4
  688.9 0.3 fusion.8
  689.2 22.7 %collective-permute-done.1 = f32[1,8,128,128]{3,2,1,0:T(8,128)S(1)} collective-permute-done((f32[1,8,128,128]{3,2,1,0:T(8,128)}, f32[1,8,128,128]{3,2,1,0:T(8,128)S(1)}, u32[]{:S(2)}, u32[]{:S(2)}) %collective-permute-start.1) | collective-permute-done | bytes 524320 | tf_op jit(solution)/shard_map/ppermute | solution.py:19
  712.0 0.0 collective-permute-done
  712.0 0.0 copy-done.2
  712.0 0.0 copy-done.3
  712.0 0.0 copy-done.4
  712.0 1.1 fusion.7
  713.0 0.0 copy-done.1
  713.1 1.6 multiply_reduce_fusion
  714.7 47.3 %psum.15 = f32[128]{0:T(128)} all-reduce(f32[128]{0:T(128)S(1)} %broadcast_multiply_fusion.1), channel_id=1, replica_groups=mesh['dom'=16,'orb'=16] {'dom'}, use_global_device_ids=true, to_apply=%region_3.4 | all-reduce | flops 128 | bytes 1024 | tf_op jit(solution)/shard_map/psum | solution.py:51
  (2 shorter events, 0.0 us)
Async XLA Ops:
  0.6 565.1 %copy-start = (f32[2048,128]{1,0:T(8,128)S(1)}, f32[2048,128]{1,0:T(8,128)}, u32[]{:S(2)}) copy-start(f32[2048,128]{1,0:T(8,128)} %param.5) | copy-start | bytes 3145732
  14.3 551.5 %copy-start.5 = (f32[128]{0:T(128)S(1)}, f32[128]{0:T(128)}, u32[]{:S(2)}) copy-start(f32[128]{0:T(128)} %param.6) | copy-start | bytes 1540
  606.7 106.4 %copy-start.1 = (f32[3072,128]{1,0:T(8,128)}, f32[3072,128]{1,0:T(8,128)S(1)}, u32[]{:S(2)}) copy-start(f32[3072,128]{1,0:T(8,128)S(1)} %get-tuple-element.17) | copy-start | bytes 4718596
  680.3 31.6 %collective-permute-start.1 = (f32[1,8,128,128]{3,2,1,0:T(8,128)}, f32[1,8,128,128]{3,2,1,0:T(8,128)S(1)}, u32[]{:S(2)}, u32[]{:S(2)}) collective-permute-start(f32[1,8,128,128]{3,2,1,0:T(8,128)} %bitcast.18), channel_id=1, source_target_pairs={{0,16},{16,32},{32,48},{48,64},{64,80},{80,96},{96,112},{112,128},... | collective-permute-start | bytes 1572872 | tf_op jit(solution)/shard_map/ppermute | solution.py:19
  680.3 31.6 %collective-permute-start = (f32[1,8,128,128]{3,2,1,0:T(8,128)S(1)}, f32[1,8,128,128]{3,2,1,0:T(8,128)S(1)}, u32[]{:S(2)}, u32[]{:S(2)}) collective-permute-start(f32[1,8,128,128]{3,2,1,0:T(8,128)S(1)} %bitcast.17), channel_id=1, source_target_pairs={{16,0},{32,16},{48,32},{64,48},{80,64},{96,80},{112,96},{128,112},... | collective-permute-start | bytes 1572872 | tf_op jit(solution)/shard_map/ppermute | solution.py:21
  688.8 23.1 %copy-start.2 = (f32[3,7,128,128]{3,2,1,0:T(8,128)S(1)}, f32[3,7,128,128]{3,2,1,0:T(8,128)}, u32[]{:S(2)}) copy-start(f32[3,7,128,128]{3,2,1,0:T(8,128)} %get-tuple-element.10) | copy-start | bytes 4128772
  688.8 23.1 %copy-start.3 = (f32[3,7,128,128]{3,2,1,0:T(8,128)S(1)}, f32[3,7,128,128]{3,2,1,0:T(8,128)}, u32[]{:S(2)}) copy-start(f32[3,7,128,128]{3,2,1,0:T(8,128)} %get-tuple-element.11) | copy-start | bytes 4128772
  688.9 23.1 %copy-start.4 = (f32[3,8,1,128]{3,2,1,0:T(1,128)S(1)}, f32[3,8,1,128]{3,2,1,0:T(1,128)}, u32[]{:S(2)}) copy-start(f32[3,8,1,128]{3,2,1,0:T(1,128)} %get-tuple-element.9) | copy-start | bytes 36868

commit v2 on v0

--- a/solution.py
+++ b/solution.py
@@ -46,7 +46,7 @@
     lap = (beside - 6.0 * field).reshape(points, local_m)
     hpsi = -0.5 * lap + potential[:, None] * rotated
     total_points = points * lax.axis_size("dom")
-    band = lax.psum(jnp.sum(rotated * hpsi, axis=0) / total_points, "dom")
+    band = jnp.sum(lax.all_gather(jnp.sum(rotated * hpsi, axis=0) / total_points, "dom"), axis=0)
     return (rotated, density, hpsi, band)
 
 

time: 474 us -> 456 us (0.962)
  blocking collectives: 118 us -> 98.9 us
    psum x1 -> x0, blocking collectives: 45.3 us -> none  [shards(): band = lax.psum(jnp.sum(rotated * hpsi, axis=0) / total_points, 'dom')]
    all_gather x0 -> x1, blocking collectives: none -> 26.3 us  [shards(): lax.all_gather(jnp.sum(rotated * hpsi, axis=0) / total_points, 'dom')]
where the time goes in v2:
time: 456 us; the launch traced here: 455 us
  waiting for transfers between devices  303 us (66%)
  blocking collectives  98.9 us (22%)
  matrix products  23.2 us (5%)
  between operations  14.1 us (3%)
  starting transfers between devices  7.8 us (2%)
  other arithmetic  4.57 us (1%)
    all_gather x1, waiting for transfers between devices, shards(): lax.all_gather(psi, 'orb', axis=1, tiled=True)  279 us
    psum x1, blocking collectives, shards(): density = lax.psum(part_density, 'orb')  72.6 us
    all_gather x1, blocking collectives, shards(): lax.all_gather(jnp.sum(rotated * hpsi, axis=0) / total_points, 'dom')  26.3 us
    dot_general x1, matrix products, shards(): jnp.dot(lax.all_gather(psi, 'orb', axis=1, tiled=True), rot, precision=la...  23.2 us
    ppermute x1, waiting for transfers between devices, with_halo(): lax.ppermute(tail, axis, [(i, (i + 1) % count) for i in range(count)])  22.7 us
  transfers between devices with their start and end apart: 3, of which 2 were waited for; matrix products, arithmetic and copies ran while one was open for 0% of the time, Pallas kernels for 0%

profile of v2, /device:TPU:32, one launch (start us, length us, event | category | flops | bytes accessed | tf_op | source)
XLA Modules:
  0.0 455.3 jit_solution(3751056321663245639)
XLA Ops:
  7.2 0.0 copy-start
  7.2 0.0 copy-start.5
  7.2 0.0 all-gather.4.cloned.1.call-start
  7.2 0.7 all-gather.4.cloned.1.call-update
  7.9 279.5 %all-gather.4.cloned.1.call-done = f32[3072,2048]{1,0:T(8,128)} async-done(((f32[3072,128]{1,0:T(8,128)}), f32[3072,2048]{1,0:T(8,128)}) %all-gather.4.cloned.1.call-update) | async-done | bytes 25165840 | tf_op jit(solution)/shard_map/all_gather | solution.py:32
  287.4 0.0 copy-done
  287.4 0.0 copy-done.5
  287.4 23.2 %fusion = (f32[3072]{0:T(1024)S(1)}, f32[3072,128]{1,0:T(8,128)S(1)}) fusion(f32[128]{0:T(128)S(1)} %copy-done.5, f32[3072,2048]{1,0:T(8,128)} %all-gather.4.cloned.1.call-done, f32[2048,128]{1,0:T(8,128)S(1)} %copy-done), kind=kOutput, calls=%fused_computation.1 | convolution fusion | flops 9664852992 | bytes 27800064 | tf_op jit(solution)/shard_map/dot_general | solution.py:31
  310.7 0.0 copy-start.1
  310.7 0.7 fusion.9
  311.4 0.9 fusion.12
  312.3 1.9 fusion.10
  314.1 0.6 broadcast_multiply_fusion
  314.7 72.6 %psum.7 = f32[3072]{0:T(1024)} all-reduce(f32[3072]{0:T(1024)} %broadcast_multiply_fusion), channel_id=1, replica_groups=mesh['dom'=16,'orb'=16] {'orb'}, use_global_device_ids=true, to_apply=%region_1.0 | all-reduce | flops 3072 | bytes 24576 | tf_op jit(solution)/shard_map/psum | solution.py:39
  387.3 0.0 collective-permute-start.1
  387.3 7.8 %collective-permute-start = (f32[1,8,128,128]{3,2,1,0:T(8,128)S(1)}, f32[1,8,128,128]{3,2,1,0:T(8,128)S(1)}, u32[]{:S(2)}, u32[]{:S(2)}) collective-permute-start(f32[1,8,128,128]{3,2,1,0:T(8,128)S(1)} %bitcast.15), channel_id=1, source_target_pairs={{16,0},{32,16},{48,32},{64,48},{80,64},{96,80},{112,96},{128,112},... | collective-permute-start | bytes 1572872 | tf_op jit(solution)/shard_map/ppermute | solution.py:21
  395.1 0.7 multiply_subtract_fusion
  395.8 0.0 copy-start.2
  395.8 0.0 copy-start.3
  395.9 0.0 copy-start.4
  395.9 0.3 fusion.8
  396.2 22.7 %collective-permute-done.1 = f32[1,8,128,128]{3,2,1,0:T(8,128)S(1)} collective-permute-done((f32[1,8,128,128]{3,2,1,0:T(8,128)}, f32[1,8,128,128]{3,2,1,0:T(8,128)S(1)}, u32[]{:S(2)}, u32[]{:S(2)}) %collective-permute-start.1) | collective-permute-done | bytes 524320 | tf_op jit(solution)/shard_map/ppermute | solution.py:19
  418.9 0.0 collective-permute-done
  418.9 0.0 copy-done.2
  418.9 0.0 copy-done.3
  418.9 0.0 copy-done.4
  418.9 1.1 fusion.7
  420.0 0.0 copy-done.1
  420.0 1.6 multiply_reduce_fusion
  421.6 26.3 %all-gather.1 = f32[16,1,128]{2,1,0:T(1,128)S(1)} all-gather(f32[1,1,128]{2,1,0:T(1,128)S(1)} %multiply_bitcast_fusion), channel_id=2, replica_groups=mesh['dom'=16,'orb'=16] {'dom'}, dimensions={0}, use_global_device_ids=true | all-gather | bytes 8704 | tf_op jit(solution)/shard_map/all_gather | solution.py:49
  447.9 0.5 reduce_sum.29
  (2 shorter events, 0.0 us)
Async XLA Ops:
  7.2 280.2 %copy-start = (f32[2048,128]{1,0:T(8,128)S(1)}, f32[2048,128]{1,0:T(8,128)}, u32[]{:S(2)}) copy-start(f32[2048,128]{1,0:T(8,128)} %param.5) | copy-start | bytes 3145732
  7.2 280.2 %copy-start.5 = (f32[128]{0:T(128)S(1)}, f32[128]{0:T(128)}, u32[]{:S(2)}) copy-start(f32[128]{0:T(128)} %param.6) | copy-start | bytes 1540
  7.2 280.2 %all-gather.4.cloned.1.call-start = ((), (), s32[]{:S(2)}) async-start(), calls=%async_computation | async-start | bytes 26738688 | tf_op jit(solution)/shard_map/all_gather | solution.py:32
  310.7 109.4 %copy-start.1 = (f32[3072,128]{1,0:T(8,128)}, f32[3072,128]{1,0:T(8,128)S(1)}, u32[]{:S(2)}) copy-start(f32[3072,128]{1,0:T(8,128)S(1)} %get-tuple-element.17) | copy-start | bytes 4718596
  387.3 31.6 %collective-permute-start.1 = (f32[1,8,128,128]{3,2,1,0:T(8,128)}, f32[1,8,128,128]{3,2,1,0:T(8,128)S(1)}, u32[]{:S(2)}, u32[]{:S(2)}) collective-permute-start(f32[1,8,128,128]{3,2,1,0:T(8,128)} %bitcast.16), channel_id=1, source_target_pairs={{0,16},{16,32},{32,48},{48,64},{64,80},{80,96},{96,112},{112,128},... | collective-permute-start | bytes 1572872 | tf_op jit(solution)/shard_map/ppermute | solution.py:19
  387.3 31.6 %collective-permute-start = (f32[1,8,128,128]{3,2,1,0:T(8,128)S(1)}, f32[1,8,128,128]{3,2,1,0:T(8,128)S(1)}, u32[]{:S(2)}, u32[]{:S(2)}) collective-permute-start(f32[1,8,128,128]{3,2,1,0:T(8,128)S(1)} %bitcast.15), channel_id=1, source_target_pairs={{16,0},{32,16},{48,32},{64,48},{80,64},{96,80},{112,96},{128,112},... | collective-permute-start | bytes 1572872 | tf_op jit(solution)/shard_map/ppermute | solution.py:21
  395.8 23.1 %copy-start.2 = (f32[3,7,128,128]{3,2,1,0:T(8,128)S(1)}, f32[3,7,128,128]{3,2,1,0:T(8,128)}, u32[]{:S(2)}) copy-start(f32[3,7,128,128]{3,2,1,0:T(8,128)} %get-tuple-element.10) | copy-start | bytes 4128772
  395.8 23.1 %copy-start.3 = (f32[3,7,128,128]{3,2,1,0:T(8,128)S(1)}, f32[3,7,128,128]{3,2,1,0:T(8,128)}, u32[]{:S(2)}) copy-start(f32[3,7,128,128]{3,2,1,0:T(8,128)} %get-tuple-element.11) | copy-start | bytes 4128772
  395.9 23.1 %copy-start.4 = (f32[3,8,1,128]{3,2,1,0:T(1,128)S(1)}, f32[3,8,1,128]{3,2,1,0:T(1,128)}, u32[]{:S(2)}) copy-start(f32[3,8,1,128]{3,2,1,0:T(1,128)} %get-tuple-element.9) | copy-start | bytes 36868
Sparse Core Ops, SparseCore 0:
  9.7 277.6 all-gather.3
